TPU v7x, 256 devices: a whole 4x4x8 slice. The times are simulated.
256 devices in a mesh: worker: 16 (over x, z_hi, core), fsdp: 16 (over z_lo, y).
Axes of the slice: x: 4, y: 4, z: 8 (z_hi: 2, z_lo: 4; z = z_hi * 4 + z_lo), core: 2. Of those that a mesh axis runs over, the one named last changes fastest.
Arguments:
- inputs: bfloat16 [16, 4096, 8192], P('worker', 'fsdp'), may hold values from -6 to 6
- output_grads: bfloat16 [16, 4096, 1024], P('worker', 'fsdp'), may hold values from -0.25 to 0.25
- local_params: float32 [16, 8192, 1024], P('worker', 'fsdp'), may hold values from -6 to 6
- first_moment: float32 [16, 8192, 1024], P('worker', 'fsdp'), may hold values from -4 to 4
- second_moment: float32 [16, 8192, 1024], P('worker', 'fsdp'), may hold values from 0.01 to 0.1
- global_params: float32 [8192, 1024], P(('fsdp', 'worker')), may hold values from -6 to 6
- momentum: float32 [8192, 1024], P(('fsdp', 'worker')), may hold values from -6 to 6
Outputs:
- new_params: float32 [8192, 1024], P('fsdp')
- new_momentum: float32 [8192, 1024], P(('fsdp', 'worker'))
All inputs are finite; a program needn't handle non-finite values.
Results may differ from a plain program's by a relative error of at most 0.0015.
Values may be sent and summed in bfloat16 or wider, within the bound.
A program may use at most 128 MiB of HBM per device.

v0:
```python
import jax
import jax.numpy as jnp
from jax import lax
from jax.sharding import PartitionSpec as P

beta_first = 0.8
beta_second = 0.9
inner_rate = 0.15
weight_decay = 0.1
adam_epsilon = 1e-08
outer_rate = 0.7
momentum_coef = 0.9
inner_count = 50


def shards(
    inputs, output_grads, local_params, first_moment, second_moment, global_params, momentum
):
    features = inputs[0]
    cotangents = output_grads[0]
    params = local_params[0]
    gradient = lax.psum_scatter(
        lax.dot_general(
            features, cotangents, (((0,), (0,)), ((), ())), preferred_element_type=jnp.float32
        ).astype(jnp.bfloat16),
        "fsdp",
        scatter_dimension=0,
        tiled=True,
    ).astype(jnp.float32)
    moment_one = beta_first * first_moment[0] + (1.0 - beta_first) * gradient
    moment_two = beta_second * second_moment[0] + (1.0 - beta_second) * gradient * gradient
    first_correction = 1.0 - beta_first**inner_count
    second_correction = 1.0 - beta_second**inner_count
    ratio = (
        moment_one / first_correction / (jnp.sqrt(moment_two / second_correction) + adam_epsilon)
    )
    stepped = params - inner_rate * (ratio + weight_decay * params)
    replicas = lax.axis_size("worker")
    anchor, moment_rows = (
        lax.all_gather(global_params, "worker", axis=0, tiled=True),
        lax.all_gather(momentum, "worker", axis=0, tiled=True),
    )
    pseudo_grad = anchor - stepped
    outer_grad = lax.psum(pseudo_grad, "worker") / replicas
    moment_full = momentum_coef * moment_rows + outer_grad
    fresh_rows = anchor - outer_rate * (outer_grad + momentum_coef * moment_full)
    share_rows = global_params.shape[0]
    worker_index = lax.axis_index("worker")
    own_moment = lax.dynamic_slice_in_dim(moment_full, worker_index * share_rows, share_rows, 0)
    return (fresh_rows, own_moment)


def solution(mesh):
    return jax.shard_map(
        shards,
        mesh=mesh,
        in_specs=(
            P("worker", "fsdp", None),
            P("worker", "fsdp", None),
            P("worker", "fsdp", None),
            P("worker", "fsdp", None),
            P("worker", "fsdp", None),
            P(("fsdp", "worker"), None),
            P(("fsdp", "worker"), None),
        ),
        out_specs=(P("fsdp", None), P(("fsdp", "worker"), None)),
        check_vma=False,
    )
```

profile of v0, /device:TPU:1, one launch (start us, length us, event | category | flops | bytes accessed | tf_op | source)
XLA Modules:
  0.0 501.1 jit_solution(11412425260126326226)
XLA Ops:
  8.0 0.0 copy-start
  8.0 0.0 all-gather.3.cloned.1.call-start
  8.1 0.7 all-gather.3.cloned.1.call-update
  8.7 0.0 reduce-scatter.2.cloned.1.call-start
  8.8 0.2 copy-done
  9.0 10.5 %convolution_convert_fusion = bf16[8192,1024]{1,0:T(8,128)(2,1)} fusion(bf16[1,256,8192]{2,1,0:T(8,128)(2,1)} %param.7, bf16[1,256,1024]{2,1,0:T(8,128)(2,1)S(1)} %copy-done), kind=kOutput, calls=%fused_computation | convolution fusion | flops 4303355904 | bytes 21495808 | tf_op jit(solution)/shard_map/dot_general | solution.py:23
  19.5 0.0 copy-start.2
  19.5 0.0 reduce-scatter.2.cloned.1.call-update
  19.5 0.0 all-gather.5.cloned.1.call-start
  19.6 0.7 all-gather.5.cloned.1.call-update
  20.3 0.0 all-reduce.2.cloned.1.call-start
  20.3 58.6 %all-gather.3.cloned.1.call-done = f32[512,1024]{1,0:T(8,128)} async-done(((f32[32,1024]{1,0:T(8,128)}), f32[512,1024]{1,0:T(8,128)}) %all-gather.3.cloned.1.call-update) | async-done | bytes 2097168 | tf_op jit(solution)/shard_map/all_gather | solution.py:40
  79.0 138.6 %reduce-scatter.2.cloned.1.call-done = bf16[512,1024]{1,0:T(8,128)(2,1)} async-done(((bf16[8192,1024]{1,0:T(8,128)(2,1)}), bf16[512,1024]{1,0:T(8,128)(2,1)}) %reduce-scatter.2.cloned.1.call-update) | async-done | bytes 1048592 | tf_op jit(solution)/shard_map/reduce_scatter | solution.py:22
  217.6 0.0 copy-done.2
  217.6 6.2 %fusion.7 = f32[512,1024]{1,0:T(8,128)} fusion(f32[512,1024]{1,0:T(8,128)} %all-gather.3.cloned.1.call-done, bf16[512,1024]{1,0:T(8,128)(2,1)} %reduce-scatter.2.cloned.1.call-done, f32[1,512,1024]{2,1,0:T(8,128)S(1)} %copy-done.2, f32[1,512,1024]{2,1,0:T(8,128)} %param.11, f32[1,512,1024]{2,1,0:T(8,128)} %param.10), kind=kLoop, calls=%fused_computation.10 | loop fusion | flops 8912896 | bytes 11534336 | tf_op jit(solution)/shard_map/sub | solution.py:43
  223.8 0.0 copy-start.1
  223.8 0.0 all-reduce.2.cloned.1.call-update
  223.8 68.9 %all-gather.5.cloned.1.call-done = f32[512,1024]{1,0:T(8,128)} async-done(((f32[32,1024]{1,0:T(8,128)}), f32[512,1024]{1,0:T(8,128)}) %all-gather.5.cloned.1.call-update) | async-done | bytes 2097168 | tf_op jit(solution)/shard_map/all_gather | solution.py:41
  292.7 196.3 %all-reduce.2.cloned.1.call-done = f32[512,1024]{1,0:T(8,128)} async-done(((f32[512,1024]{1,0:T(8,128)}), f32[512,1024]{1,0:T(8,128)}) %all-reduce.2.cloned.1.call-update) | async-done | bytes 2097168 | tf_op jit(solution)/shard_map/psum | solution.py:44
  489.0 0.0 copy-done.1
  489.0 4.3 multiply_add_fusion
  493.3 0.7 constant_dynamic-slice_fusion
Async XLA Ops:
  8.0 1.0 copy-start
  8.0 70.9 %all-gather.3.cloned.1.call-start = ((), (), s32[]{:S(2)}) async-start(), calls=%async_computation.1 | async-start | bytes 2228224 | tf_op jit(solution)/shard_map/all_gather | solution.py:40
  8.7 208.8 %reduce-scatter.2.cloned.1.call-start = ((), (), s32[]{:S(2)}) async-start(), calls=%async_computation.2 | async-start | bytes 17825792 | tf_op jit(solution)/shard_map/reduce_scatter | solution.py:22
  19.5 198.1 %copy-start.2 = (f32[1,512,1024]{2,1,0:T(8,128)S(1)}, f32[1,512,1024]{2,1,0:T(8,128)}, u32[]{:S(2)}) copy-start(f32[1,512,1024]{2,1,0:T(8,128)} %param.9) | copy-start | bytes 6291460
  19.5 273.2 %all-gather.5.cloned.1.call-start = ((), (), s32[]{:S(2)}) async-start(), calls=%async_computation.4 | async-start | bytes 2228224 | tf_op jit(solution)/shard_map/all_gather | solution.py:41
  20.3 468.7 %all-reduce.2.cloned.1.call-start = ((), (), s32[]{:S(2)}) async-start(), calls=%async_computation.3 | async-start | bytes 4194304 | tf_op jit(solution)/shard_map/psum | solution.py:44
  223.8 265.2 %copy-start.1 = (f32[512,1024]{1,0:T(8,128)S(1)}, f32[512,1024]{1,0:T(8,128)}, u32[]{:S(2)}) copy-start(f32[512,1024]{1,0:T(8,128)} %all-gather.3.cloned.1.call-done) | copy-start | bytes 6291460
Sparse Core Ops, SparseCore 0:
  11.5 67.3 all-gather.2
  81.6 211.0 all-gather.4
  295.9 192.9 all-reduce.1
Sparse Core Ops, SparseCore 1:
  19.6 197.9 reduce-scatter.1
where the time goes:
time: 506 us; the launch traced here: 501 us
  waiting for transfers between devices  464 us (92%)
  between operations  15.2 us (3%)
  matrix products  10.5 us (2%)
  other arithmetic  10.5 us (2%)
    psum x1, waiting for transfers between devices, shards(): outer_grad = lax.psum(pseudo_grad, 'worker') / replicas  196 us
    reduce_scatter x1, waiting for transfers between devices, shards(): lax.psum_scatter(lax.dot_general(features, cotangents, (((0,), (0,)), (()...  139 us
    all_gather x1, waiting for transfers between devices, shards(): lax.all_gather(momentum, 'worker', axis=0, tiled=True)  68.9 us
    all_gather x1, waiting for transfers between devices, shards(): lax.all_gather(global_params, 'worker', axis=0, tiled=True)  58.6 us
    dot_general x1, matrix products, shards(): lax.dot_general(features, cotangents, (((0,), (0,)), ((), ())), preferred...  10.5 us
  transfers between devices with their start and end apart: 4, of which 4 were waited for; matrix products, arithmetic and copies ran while one was open for 3% of the time, Pallas kernels for 0%

commit v1 on v0

v1 whole, which is shorter than its diff:
```python
import jax
import jax.numpy as jnp
from jax import lax
from jax.experimental import pallas as pl
from jax.experimental.pallas import tpu as pltpu
from jax.sharding import PartitionSpec as P

beta_first = 0.8
beta_second = 0.9
inner_rate = 0.15
weight_decay = 0.1
adam_epsilon = 1e-08
outer_rate = 0.7
momentum_coef = 0.9
inner_count = 50

MESH = pl.DeviceIdType.MESH
NX, NH, NC = 4, 2, 2
NZ, NY = 4, 4
NQ = 4


def kernel(
    x_hbm, g_hbm, lp_hbm, m1_hbm, m2_hbm, gp_hbm, mo_hbm,
    out_hbm, newm_hbm,
    xr, gr, sb, rz, lp, m1, m2, pf, sh, rc, tt, rx, uu, rh, gp, mm, np_, mn,
    xs_s, xs_r, xl, gs_s, gs_r, gl, z_s, z_r, ld, hl, hs_s, hs_r,
    rc_s, rc_r, rx_s, rx_r, rh_s, rh_r, nx_s, nx_r, nc_s, nc_r, od, md,
):
    tok, rows = xr.shape[1] // NY, xr.shape[2]
    wide = gr.shape[2]
    share = gp.shape[1]
    w, f = lax.axis_index("worker"), lax.axis_index("fsdp")
    x, h, c = w // (NH * NC), (w // NC) % NH, w % NC
    z, y = f // NY, f % NY

    def dev(x=x, h=h, c=c, z=z, y=y):
        return {"worker": (x * NH + h) * NC + c, "fsdp": z * NY + y}

    def remote(src, dst, send, recv, to):
        return pltpu.make_async_remote_copy(
            src_ref=src, dst_ref=dst, send_sem=send, recv_sem=recv, device_id=to, device_id_type=MESH
        )

    def cols(q):
        return pl.ds(pl.multiple_of(q * wide, wide), wide)

    order = [3 * (1 - z // 2), (3 * z + 2) % 5, 1 + z % 2, z]
    steps = [1 - 2 * (z // 2), 1 - 2 * (z % 2), 1 - 2 * (z // 2)]
    middle = (z == 1) | (z == 2)

    here = []
    for q in range(NQ):
        here.append(pltpu.make_async_copy(
            g_hbm.at[:, cols(q)], gr.at[q, pl.ds(pl.multiple_of(y * tok, tok), tok)], gl.at[q]))
    for k in range(NZ):
        b = order[k]
        here.append(pltpu.make_async_copy(
            x_hbm.at[:, pl.ds(pl.multiple_of((b * NY + y) * rows, rows), rows)],
            xr.at[b, pl.ds(pl.multiple_of(y * tok, tok), tok)], xl.at[k]))
    loads = [pltpu.make_async_copy(a, v, ld.at[i]) for i, (a, v) in enumerate(
        ((lp_hbm, lp), (m1_hbm, m1), (m2_hbm, m2)))]
    owns = [pltpu.make_async_copy(a, v.at[h], hl.at[i]) for i, (a, v) in enumerate(((gp_hbm, gp), (mo_hbm, mm)))]
    for copy in here + owns + loads:
        copy.start()

    barrier = pltpu.get_barrier_semaphore()
    peers = [dev(y=(y + j) % NY) for j in range(1, NY)]
    peers += [dev(x=(x + j) % NX) for j in range(1, NX)]
    peers += [dev(z=(z + 1) % NZ), dev(z=(z + NZ - 1) % NZ), dev(h=1 - h), dev(c=1 - c)]
    for peer in peers:
        pl.semaphore_signal(barrier, inc=1, device_id=peer, device_id_type=MESH)
    pl.semaphore_wait(barrier, len(peers))

    def x_copy(k, j):
        b, to = order[k], (y + j) % NY
        return remote(
            x_hbm.at[:, pl.ds(pl.multiple_of((b * NY + to) * rows, rows), rows)],
            xr.at[b, pl.ds(pl.multiple_of(y * tok, tok), tok)],
            xs_s.at[k, j - 1], xs_r.at[k, j - 1], dev(y=to))

    def g_copy(q, j):
        return remote(
            g_hbm.at[:, cols(q)], gr.at[q, pl.ds(pl.multiple_of(y * tok, tok), tok)],
            gs_s.at[q, j - 1], gs_r.at[q, j - 1], dev(y=(y + j) % NY))

    near = (1, NY - 1, 2)
    for j in near:
        g_copy(0, j).start()
    for j in near:
        x_copy(0, j).start()
    for q in range(1, NQ):
        for j in near:
            g_copy(q, j).start()
    for k in range(1, NZ):
        for j in near:
            x_copy(k, j).start()
    swaps = [remote(a, v.at[h], hs_s.at[i], hs_r.at[i], dev(h=1 - h)) for i, (a, v) in enumerate(
        ((gp_hbm, gp), (mo_hbm, mm)))]
    for copy in swaps:
        copy.start()

    def product(b, q):
        return lax.dot_general(
            xr[b], gr[q], (((0,), (0,)), ((), ())), preferred_element_type=jnp.float32)

    def z_copy(k, q, b, step):
        slot = (1 - step) // 2
        return remote(sb.at[k, q], rz.at[slot, b, q], z_s.at[k, q], z_r.at[slot, b, q], dev(z=z + step))

    def arrived(slot, b, q):
        remote(rz.at[slot, b, q], rz.at[slot, b, q], z_s.at[0, q], z_r.at[slot, b, q], dev(z=(z + 1) % NZ)).wait_recv()

    for k in range(NZ - 1):
        b, step = order[k], steps[k]
        here[NQ + k].wait()
        for j in near:
            x_copy(k, j).wait_recv()

        def send_piece(q, _, k=k, b=b, step=step):
            if k == 0:
                pltpu.make_async_copy(
                    g_hbm.at[:, cols(q)], gr.at[q, pl.ds(pl.multiple_of(y * tok, tok), tok)], gl.at[q]).wait()
                for j in near:
                    g_copy(q, j).wait_recv()
            part = product(b, q)

            @pl.when(middle)
            def _():
                pf[q] = part
                slot = (1 - step) // 2
                arrived(slot, b, q)
                sb[k, q] = (pf[q] + rz[slot, b, q].astype(jnp.float32)).astype(jnp.bfloat16)

            @pl.when(jnp.logical_not(middle))
            def _():
                sb[k, q] = part.astype(jnp.bfloat16)

            z_copy(k, q, b, step).start()
            return 0

        lax.fori_loop(0, NQ, send_piece, 0)

    here[NQ + NZ - 1].wait()
    for j in near:
        x_copy(NZ - 1, j).wait_recv()

    def own_piece(q, _):
        pf[q] = product(z, q)
        return 0

    lax.fori_loop(0, NQ, own_piece, 0)
    for copy in loads + owns:
        copy.wait()
    for copy in swaps:
        copy.wait_recv()

    first_correction = 1.0 - beta_first**inner_count
    second_correction = 1.0 - beta_second**inner_count

    def rc_copy(q):
        return remote(sh.at[q, 1 - c], rc.at[q], rc_s.at[q], rc_r.at[q], dev(c=1 - c))

    def rx_copy(q, j):
        to = (x + j) % NX
        return remote(tt.at[q, to], rx.at[q, j - 1], rx_s.at[q, j - 1], rx_r.at[q, j - 1], dev(x=to))

    def rh_copy(q):
        return remote(uu.at[q], rh.at[q], rh_s.at[q], rh_r.at[q], dev(h=1 - h))

    def nx_copy(q, j):
        return remote(
            np_.at[q, c, x], np_.at[q, c, x], nx_s.at[q, j - 1], nx_r.at[q, j - 1], dev(x=(x + j) % NX))

    def nx_wait(q, j):
        remote(np_.at[q, c, (x + NX - j) % NX], np_.at[q, c, (x + NX - j) % NX],
               nx_s.at[q, j - 1], nx_r.at[q, j - 1], dev(x=(x + j) % NX)).wait_recv()

    def nc_copy(q):
        return remote(np_.at[q, c], np_.at[q, c], nc_s.at[q], nc_r.at[q], dev(c=1 - c))

    def nc_wait(q):
        remote(np_.at[q, 1 - c], np_.at[q, 1 - c], nc_s.at[q], nc_r.at[q], dev(c=1 - c)).wait_recv()

    def out_copy(q, i):
        return pltpu.make_async_copy(np_.at[q, i], out_hbm.at[:, :, i, :, cols(q)], od.at[q, i])

    def m_copy(q):
        return pltpu.make_async_copy(mn.at[q, h], newm_hbm.at[:, cols(q)], md.at[q])

    def adam(q):
        @pl.when(z > 0)
        def _():
            arrived(0, z, q)
            pf[q] = pf[q] + rz[0, z, q].astype(jnp.float32)

        @pl.when(z < NZ - 1)
        def _():
            arrived(1, z, q)
            pf[q] = pf[q] + rz[1, z, q].astype(jnp.float32)

        def block(i, _):
            at = pl.ds(pl.multiple_of(i * share, share), share)
            grad = pf[q, at]
            moment_one = beta_first * m1[at, cols(q)] + (1.0 - beta_first) * grad
            moment_two = beta_second * m2[at, cols(q)] + (1.0 - beta_second) * grad * grad
            params = lp[at, cols(q)]
            ratio = moment_one / first_correction / (jnp.sqrt(moment_two / second_correction) + adam_epsilon)
            sh[q, i % NC, i // NC] = params - inner_rate * (ratio + weight_decay * params)
            return 0

        lax.fori_loop(0, rows // share, block, 0)
        rc_copy(q).start()

    def to_x(q):
        rc_copy(q).wait_recv()
        total = sh[q, c] + rc[q]
        tt[q] = total.reshape(tt.shape[1:])
        for j in near:
            rx_copy(q, j).start()

    def to_h(q):
        for j in near:
            rx_copy(q, j).wait_recv()
        uu[q] = tt[q, x] + rx[q, 0] + rx[q, 1] + rx[q, 2]
        rh_copy(q).start()

    def update(q):
        rh_copy(q).wait_recv()
        mean = (uu[q] + rh[q]) * (1.0 / (NX * NH * NC))
        anchor = gp[:, :, cols(q)]
        outer_grad = anchor - mean
        fresh = momentum_coef * mm[:, :, cols(q)] + outer_grad
        mn[q] = fresh
        np_[q, c, x] = anchor - outer_rate * (outer_grad + momentum_coef * fresh)
        for j in near:
            nx_copy(q, j).start()
        m_copy(q).start()

    def to_core(q):
        for j in near:
            nx_wait(q, j)
        nc_copy(q).start()
        out_copy(q, c).start()

    def finish(q):
        nc_wait(q)
        out_copy(q, 1 - c).start()

    def turn(t, _):
        for lag, stage in ((0, adam), (0, to_x), (1, to_h), (2, update), (3, to_core), (4, finish)):
            @pl.when((t >= lag) & (t < NQ + lag))
            def _(lag=lag, stage=stage):
                stage(t - lag)
        return 0

    lax.fori_loop(0, NQ + 4, turn, 0)

    def drain(q, _):
        for j in near:
            g_copy(q, j).wait_send()
            rx_copy(q, j).wait_send()
            nx_copy(q, j).wait_send()
        for k in range(NZ - 1):
            z_copy(k, q, order[k], steps[k]).wait_send()
        rc_copy(q).wait_send()
        rh_copy(q).wait_send()
        nc_copy(q).wait_send()
        out_copy(q, c).wait()
        out_copy(q, 1 - c).wait()
        m_copy(q).wait()
        return 0

    lax.fori_loop(0, NQ, drain, 0)
    for k in range(NZ):
        for j in near:
            x_copy(k, j).wait_send()
    for copy in swaps:
        copy.wait_send()


def shards(
    inputs, output_grads, local_params, first_moment, second_moment, global_params, momentum
):
    tok, width = inputs.shape[1], output_grads.shape[2]
    rows, share = local_params.shape[1], global_params.shape[0]
    wide = width // NQ
    f32, bf16 = jnp.float32, jnp.bfloat16
    dma = pltpu.SemaphoreType.DMA
    ins = (inputs[0], output_grads[0], local_params[0], first_moment[0], second_moment[0], global_params, momentum)
    own = (NX, NH, share, wide)
    new_params, new_momentum = pl.pallas_call(
        kernel,
        out_shape=(
            jax.ShapeDtypeStruct((NX, NH, NC, share, width), f32),
            jax.ShapeDtypeStruct((share, width), f32),
        ),
        in_specs=[pl.BlockSpec(memory_space=pl.ANY)] * len(ins),
        out_specs=(pl.BlockSpec(memory_space=pl.ANY),) * 2,
        scratch_shapes=[
            pltpu.VMEM((NZ, NY * tok, rows), bf16),
            pltpu.VMEM((NQ, NY * tok, wide), bf16),
            pltpu.VMEM((NZ - 1, NQ, rows, wide), bf16),
            pltpu.VMEM((2, NZ, NQ, rows, wide), bf16),
            pltpu.VMEM((rows, width), f32),
            pltpu.VMEM((rows, width), f32),
            pltpu.VMEM((rows, width), f32),
            pltpu.VMEM((NQ, rows, wide), f32),
            pltpu.VMEM((NQ, NC, NX * NH, share, wide), f32),
            pltpu.VMEM((NQ, NX * NH, share, wide), f32),
            pltpu.VMEM((NQ,) + own, f32),
            pltpu.VMEM((NQ, NX - 1, NH, share, wide), f32),
            pltpu.VMEM((NQ, NH, share, wide), f32),
            pltpu.VMEM((NQ, NH, share, wide), f32),
            pltpu.VMEM((NH, share, width), f32),
            pltpu.VMEM((NH, share, width), f32),
            pltpu.VMEM((NQ, NC) + own, f32),
            pltpu.VMEM((NQ, NH, share, wide), f32),
            dma((NZ, NY - 1)), dma((NZ, NY - 1)), dma((NZ,)),
            dma((NQ, NY - 1)), dma((NQ, NY - 1)), dma((NQ,)),
            dma((NZ - 1, NQ)), dma((2, NZ, NQ)), dma((3,)), dma((2,)), dma((2,)), dma((2,)),
            dma((NQ,)), dma((NQ,)), dma((NQ, NX - 1)), dma((NQ, NX - 1)), dma((NQ,)), dma((NQ,)),
            dma((NQ, NX - 1)), dma((NQ, NX - 1)), dma((NQ,)), dma((NQ,)), dma((NQ, NC)), dma((NQ,)),
        ],
        compiler_params=pltpu.CompilerParams(
            collective_id=0, has_side_effects=True, vmem_limit_bytes=56 << 20
        ),
    )(*ins)
    return (new_params.reshape(rows, width), new_momentum)


def solution(mesh):
    return jax.shard_map(
        shards,
        mesh=mesh,
        in_specs=(
            P("worker", "fsdp", None),
            P("worker", "fsdp", None),
            P("worker", "fsdp", None),
            P("worker", "fsdp", None),
            P("worker", "fsdp", None),
            P(("fsdp", "worker"), None),
            P(("fsdp", "worker"), None),
        ),
        out_specs=(P("fsdp", None), P(("fsdp", "worker"), None)),
        check_vma=False,
    )
```

time: 506 us -> 138 us (0.27)
  waiting for transfers between devices: 464 us -> 0 us
  Pallas kernels: 0 us -> 133 us
  between operations: 15.2 us -> 0.65 us
  matrix products: 10.5 us -> 0 us
  other arithmetic: 10.5 us -> 0 us
    psum x1 -> x0, waiting for transfers between devices: 196 us -> none  [shards(): outer_grad = lax.psum(pseudo_grad, 'worker') / replicas]
    reduce_scatter x1 -> x0, waiting for transfers between devices: 139 us -> none  [shards(): lax.psum_scatter(lax.dot_general(features, cotangents, (((0,), (0,)), (()...]
    pallas_call x0 -> x1, Pallas kernels: none -> 133 us  [shards(): pl.pallas_call(kernel, out_shape=(jax.ShapeDtypeStruct((NX, NH, NC, share...]
    all_gather x2 -> x0, waiting for transfers between devices: 128 us -> none  [the longest x1 68.9 us: shards(): lax.all_gather(momentum, 'worker', axis=0, tiled=True)]
    dot_general x1 -> x0, matrix products: 10.5 us -> none  [shards(): lax.dot_general(features, cotangents, (((0,), (0,)), ((), ())), preferred...]
    sub x1 -> x0, other arithmetic: 6.2 us -> none  [shards(): pseudo_grad = anchor - stepped]
  transfers between devices with their start and end apart: 4 -> 0, of which waited for: 4 -> 0; matrix products, arithmetic and copies ran while one was open for 3% -> 0% of each run, Pallas kernels for 0% -> 0%
where the time goes in v1:
time: 138 us
  Pallas kernels  133 us (96%)
  local copies, waits for them, and re-layouts  3.85 us (3%)
    pallas_call x1, Pallas kernels, shards(): pl.pallas_call(kernel, out_shape=(jax.ShapeDtypeStruct((NX, NH, NC, share...  133 us
    unnamed x4, local copies, waits for them, and re-layouts  3.85 us

profile of v1, /device:TPU:1, one launch (start us, length us, event | category | flops | bytes accessed | tf_op | source)
XLA Modules:
  0.0 137.8 jit_solution(17204383760639040403)
XLA Ops:
  0.6 133.3 %shard_map.86 = (f32[4,2,2,32,1024]{4,3,2,1,0:T(8,128)}, f32[32,1024]{1,0:T(8,128)}) custom-call(bf16[256,8192]{1,0:T(8,128)(2,1)} %bitcast.6, bf16[256,1024]{1,0:T(8,128)(2,1)} %bitcast.11, f32[512,1024]{1,0:T(8,128)} %bitcast.8, f32[512,1024]{1,0:T(8,128)} %bitcast.9, f32[512,1024]{1,0:T(8,128)} %bitcast.10, f32[32,1024]{1,0:T(8,128)} %gp_hbm.1, ...), custom_call_target="tpu_custom_call" | custom-call | tf_op jit(solution)/shard_map/pallas_call | solution.py:292
  133.9 0.0 copy-start
  133.9 3.2 %copy.11 = f32[512,1024]{1,0:T(8,128)} copy(f32[512,1024]{1,0:T(8,128)} %bitcast.7) | data formatting | bytes 4194304
  137.1 0.0 copy-done
  137.1 0.7 copy.12
Async XLA Ops:
  133.9 3.2 %copy-start = (f32[32,1024]{1,0:T(8,128)S(1)}, f32[32,1024]{1,0:T(8,128)}, u32[]{:S(2)}) copy-start(f32[32,1024]{1,0:T(8,128)} %get-tuple-element.9) | copy-start | bytes 393220

commit v2 on v1

--- a/solution.py
+++ b/solution.py
@@ -23,8 +23,8 @@
 def kernel(
     x_hbm, g_hbm, lp_hbm, m1_hbm, m2_hbm, gp_hbm, mo_hbm,
     out_hbm, newm_hbm,
-    xr, gr, sb, rz, lp, m1, m2, pf, sh, rc, tt, rx, uu, rh, gp, mm, np_, mn,
-    xs_s, xs_r, xl, gs_s, gs_r, gl, z_s, z_r, ld, hl, hs_s, hs_r,
+    xv, xr, gr, sb, rz, lp, m1, m2, pf, sh, rc, tt, rx, uu, rh, gp, mm, np_, mn,
+    xw, xs_s, xs_r, xl, gs_s, gs_r, gl, z_s, z_r, ld, hl, hs_s, hs_r,
     rc_s, rc_r, rx_s, rx_r, rh_s, rh_r, nx_s, nx_r, nc_s, nc_r, od, md,
 ):
     tok, rows = xr.shape[1] // NY, xr.shape[2]
@@ -49,6 +49,13 @@
     steps = [1 - 2 * (z // 2), 1 - 2 * (z % 2), 1 - 2 * (z // 2)]
     middle = (z == 1) | (z == 2)
 
+    brought = [
+        pltpu.make_async_copy(
+            x_hbm.at[:, pl.ds(pl.multiple_of(order[k] * NY * rows, NY * rows), NY * rows)], xv.at[k], xw.at[k])
+        for k in range(NZ)
+    ]
+    for copy in brought:
+        copy.start()
     here = []
     for q in range(NQ):
         here.append(pltpu.make_async_copy(
@@ -75,7 +82,7 @@
     def x_copy(k, j):
         b, to = order[k], (y + j) % NY
         return remote(
-            x_hbm.at[:, pl.ds(pl.multiple_of((b * NY + to) * rows, rows), rows)],
+            xv.at[k, :, pl.ds(pl.multiple_of(to * rows, rows), rows)],
             xr.at[b, pl.ds(pl.multiple_of(y * tok, tok), tok)],
             xs_s.at[k, j - 1], xs_r.at[k, j - 1], dev(y=to))
 
@@ -87,12 +94,14 @@
     near = (1, NY - 1, 2)
     for j in near:
         g_copy(0, j).start()
+    brought[0].wait()
     for j in near:
         x_copy(0, j).start()
     for q in range(1, NQ):
         for j in near:
             g_copy(q, j).start()
     for k in range(1, NZ):
+        brought[k].wait()
         for j in near:
             x_copy(k, j).start()
     swaps = [remote(a, v.at[h], hs_s.at[i], hs_r.at[i], dev(h=1 - h)) for i, (a, v) in enumerate(
@@ -248,13 +257,13 @@
         out_copy(q, 1 - c).start()
 
     def turn(t, _):
-        for lag, stage in ((0, adam), (0, to_x), (1, to_h), (2, update), (3, to_core), (4, finish)):
+        for lag, stage in ((0, adam), (1, to_x), (2, to_h), (3, update), (4, to_core), (5, finish)):
             @pl.when((t >= lag) & (t < NQ + lag))
             def _(lag=lag, stage=stage):
                 stage(t - lag)
         return 0
 
-    lax.fori_loop(0, NQ + 4, turn, 0)
+    lax.fori_loop(0, NQ + 5, turn, 0)
 
     def drain(q, _):
         for j in near:
@@ -298,6 +307,7 @@
         in_specs=[pl.BlockSpec(memory_space=pl.ANY)] * len(ins),
         out_specs=(pl.BlockSpec(memory_space=pl.ANY),) * 2,
         scratch_shapes=[
+            pltpu.VMEM((NZ, tok, NY * rows), bf16),
             pltpu.VMEM((NZ, NY * tok, rows), bf16),
             pltpu.VMEM((NQ, NY * tok, wide), bf16),
             pltpu.VMEM((NZ - 1, NQ, rows, wide), bf16),
@@ -316,7 +326,7 @@
             pltpu.VMEM((NH, share, width), f32),
             pltpu.VMEM((NQ, NC) + own, f32),
             pltpu.VMEM((NQ, NH, share, wide), f32),
-            dma((NZ, NY - 1)), dma((NZ, NY - 1)), dma((NZ,)),
+            dma((NZ,)), dma((NZ, NY - 1)), dma((NZ, NY - 1)), dma((NZ,)),
             dma((NQ, NY - 1)), dma((NQ, NY - 1)), dma((NQ,)),
             dma((NZ - 1, NQ)), dma((2, NZ, NQ)), dma((3,)), dma((2,)), dma((2,)), dma((2,)),
             dma((NQ,)), dma((NQ,)), dma((NQ, NX - 1)), dma((NQ, NX - 1)), dma((NQ,)), dma((NQ,)),

time: 138 us -> 137 us (level)
  no operation moved by 1% of the time
where the time goes in v2:
time: 137 us; the launch traced here: 136 us
  Pallas kernels  132 us (96%)
  local copies, waits for them, and re-layouts  3.85 us (3%)
    pallas_call x1, Pallas kernels, shards(): pl.pallas_call(kernel, out_shape=(jax.ShapeDtypeStruct((NX, NH, NC, share...  132 us
    unnamed x4, local copies, waits for them, and re-layouts  3.85 us

profile of v2, /device:TPU:1, one launch (start us, length us, event | category | flops | bytes accessed | tf_op | source)
XLA Modules:
  0.0 136.5 jit_solution(18238196779919313878)
XLA Ops:
  0.6 132.0 %shard_map.86 = (f32[4,2,2,32,1024]{4,3,2,1,0:T(8,128)}, f32[32,1024]{1,0:T(8,128)}) custom-call(bf16[256,8192]{1,0:T(8,128)(2,1)} %bitcast.6, bf16[256,1024]{1,0:T(8,128)(2,1)} %bitcast.11, f32[512,1024]{1,0:T(8,128)} %bitcast.8, f32[512,1024]{1,0:T(8,128)} %bitcast.9, f32[512,1024]{1,0:T(8,128)} %bitcast.10, f32[32,1024]{1,0:T(8,128)} %gp_hbm.1, ...), custom_call_target="tpu_custom_call" | custom-call | tf_op jit(solution)/shard_map/pallas_call | solution.py:301
  132.6 0.0 copy-start
  132.6 3.2 %copy.11 = f32[512,1024]{1,0:T(8,128)} copy(f32[512,1024]{1,0:T(8,128)} %bitcast.7) | data formatting | bytes 4194304
  135.8 0.0 copy-done
  135.8 0.7 copy.12
Async XLA Ops:
  132.6 3.2 %copy-start = (f32[32,1024]{1,0:T(8,128)S(1)}, f32[32,1024]{1,0:T(8,128)}, u32[]{:S(2)}) copy-start(f32[32,1024]{1,0:T(8,128)} %get-tuple-element.9) | copy-start | bytes 393220
